TPU v7x, 32 devices: a whole 2x2x4 slice. The times are simulated.
32 devices in a mesh: date: 16 (over z, y, core), tile: 2 (over x).
Axes of the slice: x: 2, y: 2, z: 4, core: 2. Of those that a mesh axis runs over, the one named last changes fastest.
Arguments:
- latest_model_output: float32 [2, 24, 16, 16, 64], P(None, None, None, 'tile', 'date'), may hold values from -6 to 6
- bygone_model_outputs: float32 [64, 24, 16, 16, 64], P('date', None, None, 'tile'), may hold values from -6 to 6
- sensor_reports: float32 [64, 24, 16, 64], P('date', None, 'tile'), may hold values from -6 to 6
- input_variable_scaling: float32 [16], replicated, may hold values from 0.25 to 4
- stepahead_blur_scale: float32 [24], replicated, may hold values from 0.02 to 0.08
- bygone_annual_ordinal: int32 [64], P('date'), may hold values from 0 to 364
- launch_annual_ordinal: int32 [2], replicated, may hold values from 0 to 364
Outputs:
- analog_mean: float32 [2, 24, 16, 64], P(None, None, 'tile', 'date')
All inputs are finite; a program needn't handle non-finite values.
Results may differ from a plain program's by a relative error of at most 0.0003.
Values sent between devices are 32-bit elements; how exact they have to be, the bound alone decides.
No kernel may reach another device: no remote copies, remote signals or barrier semaphores. Data moves between devices by JAX's collectives and lax.ppermute only.
A program may use at most 128 MiB of HBM per device.

v0:
```python
import math

import jax
import jax.numpy as jnp
from jax import lax
from jax.sharding import PartitionSpec as P

WIN_HALF = 3


season_gain = 0.5


def extended(x, sides, width):
    for axis, dim in sides:
        size, length = (lax.axis_size(axis), x.shape[dim])
        up = [(i, (i + 1) % size) for i in range(size - 1)]
        down = [(j, i) for i, j in up]
        last = lax.slice_in_dim(x, length - width, length, axis=dim)
        initial = lax.slice_in_dim(x, 0, width, axis=dim)
        before = lax.ppermute(last, axis, up)
        after = lax.ppermute(initial, axis, down)
        x = jnp.concatenate([before, x, after], axis=dim)
    return x


def joined(part, axis, combine):
    gathered = jax.tree.map(lambda a: lax.all_gather(a, axis), part)

    def take(source):
        return jax.tree.map(lambda a: lax.dynamic_index_in_dim(a, source, 0, False), gathered)

    return lax.fori_loop(
        1, lax.axis_size(axis), lambda source, state: combine(state, take(source)), take(0)
    )


def season_term(calendar, today):
    return season_gain * (
        1.0 - jnp.cos(2.0 * math.pi * (calendar - today).astype(jnp.float32) / 365.0)
    )


def lead_window(diffsq, reach):
    lead_count = diffsq.shape[1]
    padded = jnp.pad(diffsq, ((0, 0), (reach, reach), (0, 0), (0, 0)))
    lead_total = padded[:, 0:lead_count]
    for offset in range(1, 2 * reach + 1):
        lead_total = lead_total + padded[:, offset : offset + lead_count]
    return lead_total


def space_window(lead_total, row_count, col_count):
    padded = jnp.pad(lead_total, [(0, 0)] * (lead_total.ndim - 1) + [(1, 1)])
    row_total = (
        padded[..., 0:row_count, :]
        + padded[..., 1 : row_count + 1, :]
        + padded[..., 2 : row_count + 2, :]
    )
    return (
        row_total[..., 0:col_count]
        + row_total[..., 1 : col_count + 1]
        + row_total[..., 2 : col_count + 2]
    )


def cycle_distance(current, bygone_sample, input_variable_scaling, calendar, today, reach):
    row_count = bygone_sample.shape[3] - 2
    col_count = bygone_sample.shape[4]
    feature_discrepancy = current[None] - bygone_sample
    diffsq = (
        jnp.sum(
            feature_discrepancy
            * feature_discrepancy
            * input_variable_scaling[None, None, :, None, None],
            axis=2,
        )
        / bygone_sample.shape[2]
    )
    totals = space_window(lead_window(diffsq, reach), row_count, col_count)
    return totals / (9.0 * (2 * reach + 1)) + season_term(calendar, today)[:, None, None, None]


def local(
    latest_model_output,
    bygone_model_outputs,
    sensor_reports,
    input_variable_scaling,
    stepahead_blur_scale,
    bygone_annual_ordinal,
    launch_annual_ordinal,
):
    gathered_amounts = lax.all_gather(latest_model_output, "date", axis=4, tiled=True)
    current = extended(gathered_amounts, (("tile", 3),), 1)
    bygone_sample = extended(bygone_model_outputs, (("tile", 3),), 1)
    per_cycle = []
    for cycle_index in range(current.shape[0]):
        per_cycle.append(
            cycle_distance(
                current[cycle_index],
                bygone_sample,
                input_variable_scaling,
                bygone_annual_ordinal,
                launch_annual_ordinal[cycle_index],
                WIN_HALF,
            )
        )
    analog_metric = jnp.stack(per_cycle, axis=0)
    local_min = jnp.min(analog_metric, axis=1)
    spread_five = stepahead_blur_scale[None, None, :, None, None]
    spread_four = stepahead_blur_scale[None, :, None, None]
    kernel = jnp.exp(-(analog_metric - local_min[:, None]) / spread_five)
    numer = jnp.sum(kernel * sensor_reports[None], axis=1)
    denom = jnp.sum(kernel, axis=1)

    def combine(left, right):
        lowest = jnp.minimum(left[0], right[0])
        left_scale = jnp.exp(-(left[0] - lowest) / spread_four)
        right_scale = jnp.exp(-(right[0] - lowest) / spread_four)
        return (
            lowest,
            left[1] * left_scale + right[1] * right_scale,
            left[2] * left_scale + right[2] * right_scale,
        )

    merged = joined((local_min, numer, denom), "date", combine)
    ratio = merged[1] / merged[2]
    width = ratio.shape[3] // lax.axis_size("date")
    start = lax.axis_index("date") * width
    return lax.dynamic_slice_in_dim(ratio, start, width, 3)


def solution(mesh):
    placed = (
        P(None, None, None, "tile", "date"),
        P("date", None, None, "tile", None),
        P("date", None, "tile", None),
        P(),
        P(),
        P("date"),
        P(),
    )
    return jax.shard_map(
        local, mesh=mesh, in_specs=placed, out_specs=P(None, None, "tile", "date"), check_vma=False
    )
```

profile of v0, /device:TPU:0, one launch (start us, length us, event | category | flops | bytes accessed | tf_op | source)
XLA Modules:
  0.0 313.2 jit_solution(5245792410823408291)
XLA Ops:
  6.5 1.9 copy.36
  8.5 7.5 %fusion.30 = (f32[4,24,16,1,64]{4,3,2,1,0:T(1,128)}, f32[4,24,16,1,64]{4,3,2,1,0:T(1,128)}) fusion(f32[4,24,16,8,64]{4,3,2,1,0:T(8,128)} %param.10), kind=kLoop, calls=%fused_computation.71 | loop fusion | bytes 1572864 | tf_op jit(solution)/shard_map/slice | solution.py:19
  16.0 5.9 %collective-permute-start.2 = (f32[4,24,16,1,64]{4,2,3,1,0:T(8,128)}, f32[4,24,16,1,64]{4,2,3,1,0:T(8,128)}, u32[]{:S(2)}, u32[]{:S(2)}) collective-permute-start(f32[4,24,16,1,64]{4,2,3,1,0:T(8,128)} %bitcast.16), channel_id=1, source_target_pairs={{0,1},{2,3},{4,5},{6,7},{8,9},{10,11},{12,13},{14,15},{16,17},{18,... | collective-permute-start | bytes 1179656 | tf_op jit(solution)/shard_map/ppermute | solution.py:21
  21.9 1.3 collective-permute-start.3
  23.7 62.8 %all-gather.8.cloned.1.call-done = f32[2,24,16,8,64]{1,3,2,0,4:T(8,128)} async-done(((f32[2,24,16,8,4]{1,3,2,0,4:T(8,128)}), f32[2,24,16,8,64]{1,3,2,0,4:T(8,128)}) %all-gather.8.cloned.1.call-update) | async-done | bytes 1572880 | tf_op jit(solution)/shard_map/all_gather | solution.py:93
  86.5 8.1 %fusion.29 = (f32[2,24,16,1,64]{1,3,2,0,4:T(1,128)S(1)}, f32[2,24,16,1,64]{1,3,2,0,4:T(1,128)S(1)}) fusion(f32[2,24,16,8,64]{1,3,2,0,4:T(8,128)} %all-gather.8.cloned.1.call-done), kind=kLoop, calls=%fused_computation.70 | loop fusion | bytes 786432 | tf_op jit(solution)/shard_map/slice | solution.py:19
  95.4 4.1 %collective-permute-start = (f32[2,24,16,1,64]{4,2,3,1,0:T(8,128)S(1)}, f32[2,24,16,1,64]{4,2,3,1,0:T(8,128)}, u32[]{:S(2)}, u32[]{:S(2)}) collective-permute-start(f32[2,24,16,1,64]{4,2,3,1,0:T(8,128)S(1)} %copy.37), channel_id=1, source_target_pairs={{0,1},{2,3},{4,5},{6,7},{8,9},{10,11},{12,13},{14,15},{16,17},{18,... | collective-permute-start | bytes 589832 | tf_op jit(solution)/shard_map/ppermute | solution.py:21
  99.5 1.8 copy.38
  101.3 1.5 collective-permute-start.1
  102.8 1.3 subtract_multiply_fusion.1
  104.0 7.2 %copy.39 = f32[2,24,16,8,64]{4,2,3,1,0:T(8,128)S(1)} copy(f32[2,24,16,8,64]{1,3,2,0,4:T(8,128)} %all-gather.8.cloned.1.call-done) | data formatting | bytes 3145728 | tf_op jit(solution)/shard_map/all_gather | solution.py:93
  111.3 3.2 %collective-permute-done.1 = f32[2,24,16,1,64]{4,2,3,1,0:T(8,128)} collective-permute-done((f32[2,24,16,1,64]{4,2,3,1,0:T(8,128)}, f32[2,24,16,1,64]{4,2,3,1,0:T(8,128)}, u32[]{:S(2)}, u32[]{:S(2)}) %collective-permute-start.1) | collective-permute-done | bytes 196640 | tf_op jit(solution)/shard_map/ppermute | solution.py:22
  114.5 1.5 pad_maximum_fusion.1
  119.0 9.2 %multiply_reduce_fusion.1 = (f32[4,24,10,64]{3,2,1,0:T(8,128)S(1)}, f32[4,24,10,64]{3,2,1,0:T(8,128)S(1)}) fusion(f32[4,24,16,1,64]{4,3,2,1,0:T(1,128)} %bitcast.6, f32[4,24,16,8,64]{4,3,2,1,0:T(8,128)S(1)} %bitcast.50, f32[4,24,16,1,64]{4,3,2,1,0:T(1,128)} %bitcast.5, f32[16]{0:T(128)S(1)} %copy-done.4, f32[24,16,10,64]{3,2,1,0:T(8,128)S(1)} %copy.40, ...), kind=kLoop, calls=%fused_computation.12 | loop fusion | flops 9707520 | bytes 6389824 | tf_op jit(solution)/shard_map/reduce_sum | solution.py:72
  132.6 42.0 %all-gather.12.cloned.1.call-done = f32[32,24,8,64]{3,2,1,0:T(8,128)} async-done(((f32[2,24,8,64]{3,2,1,0:T(8,128)}), f32[32,24,8,64]{3,2,1,0:T(8,128)}) %all-gather.12.cloned.1.call-update) | async-done | bytes 1572880 | tf_op jit(solution)/shard_map/all_gather | solution.py:28
  175.5 45.2 %all-gather.14.cloned.1.call-done = f32[32,24,8,64]{3,2,1,0:T(8,128)} async-done(((f32[2,24,8,64]{3,2,1,0:T(8,128)}), f32[32,24,8,64]{3,2,1,0:T(8,128)}) %all-gather.14.cloned.1.call-update) | async-done | bytes 1572880 | tf_op jit(solution)/shard_map/all_gather | solution.py:28
  221.6 45.0 %all-gather.10.cloned.1.call-done = f32[32,24,8,64]{3,2,1,0:T(8,128)} async-done(((f32[2,24,8,64]{3,2,1,0:T(8,128)}), f32[32,24,8,64]{3,2,1,0:T(8,128)}) %all-gather.10.cloned.1.call-update) | async-done | bytes 1572880 | tf_op jit(solution)/shard_map/all_gather | solution.py:28
  267.6 38.1 %while.19 = (s32[]{:T(128)}, f32[2,24,8,64]{3,2,1,0:T(8,128)S(1)}, f32[2,24,8,64]{3,2,1,0:T(8,128)S(1)}, f32[2,24,8,64]{3,2,1,0:T(8,128)S(1)}, f32[16,2,24,8,64]...) while((s32[]{:T(128)}, f32[2,24,8,64]{3,2,1,0:T(8,128)S(1)}, ...), condition=%wide.region_6.7_spmd, body=%wide.region_5.6_spmd.sunk | while | flops 466949 | bytes 1376607 | solution.py:33
  267.6 1.2 fusion.34
  270.1 1.2 fusion.34
  272.7 1.2 fusion.34
  275.2 1.2 fusion.34
  277.8 1.2 fusion.34
  280.3 1.2 fusion.34
  (86 shorter events, 42.4 us)
Async XLA Ops:
  6.5 16.6 %copy-start.3 = (s32[2]{0:T(128)S(1)}, s32[2]{0:T(128)}, u32[]{:S(2)}) copy-start(s32[2]{0:T(128)} %param.15) | copy-start | bytes 28
  6.5 80.0 %all-gather.8.cloned.1.call-start = ((), (), s32[]{:S(2)}) async-start(), calls=%async_computation | async-start | bytes 8912896 | tf_op jit(solution)/shard_map/all_gather | solution.py:93
  8.4 166.1 %all-gather.12.cloned.1.call-start = ((), (), s32[]{:S(2)}) async-start(), calls=%async_computation.2 | async-start | bytes 3342336 | tf_op jit(solution)/shard_map/all_gather | solution.py:28
  16.0 86.8 %copy-start.5 = (s32[4]{0:T(128)S(1)}, s32[4]{0:T(128)}, u32[]{:S(2)}) copy-start(s32[4]{0:T(128)} %param.14) | copy-start | bytes 52
  16.0 102.0 %collective-permute-start.2 = (f32[4,24,16,1,64]{4,2,3,1,0:T(8,128)}, f32[4,24,16,1,64]{4,2,3,1,0:T(8,128)}, u32[]{:S(2)}, u32[]{:S(2)}) collective-permute-start(f32[4,24,16,1,64]{4,2,3,1,0:T(8,128)} %bitcast.16), channel_id=1, source_target_pairs={{0,1},{2,3},{4,5},{6,7},{8,9},{10,11},{12,13},{14,15},{16,17},{18,... | collective-permute-start | bytes 1179656 | tf_op jit(solution)/shard_map/ppermute | solution.py:21
  21.9 96.1 %collective-permute-start.3 = (f32[4,24,16,1,64]{4,2,3,1,0:T(8,128)}, f32[4,24,16,1,64]{4,2,3,1,0:T(8,128)}, u32[]{:S(2)}, u32[]{:S(2)}) collective-permute-start(f32[4,24,16,1,64]{4,2,3,1,0:T(8,128)} %bitcast.17), channel_id=1, source_target_pairs={{1,0},{3,2},{5,4},{7,6},{9,8},{11,10},{13,12},{15,14},{17,16},{19,... | collective-permute-start | bytes 1179656 | tf_op jit(solution)/shard_map/ppermute | solution.py:22
  95.4 15.9 %collective-permute-start = (f32[2,24,16,1,64]{4,2,3,1,0:T(8,128)S(1)}, f32[2,24,16,1,64]{4,2,3,1,0:T(8,128)}, u32[]{:S(2)}, u32[]{:S(2)}) collective-permute-start(f32[2,24,16,1,64]{4,2,3,1,0:T(8,128)S(1)} %copy.37), channel_id=1, source_target_pairs={{0,1},{2,3},{4,5},{6,7},{8,9},{10,11},{12,13},{14,15},{16,17},{18,... | collective-permute-start | bytes 589832 | tf_op jit(solution)/shard_map/ppermute | solution.py:21
  101.3 13.2 %collective-permute-start.1 = (f32[2,24,16,1,64]{4,2,3,1,0:T(8,128)}, f32[2,24,16,1,64]{4,2,3,1,0:T(8,128)}, u32[]{:S(2)}, u32[]{:S(2)}) collective-permute-start(f32[2,24,16,1,64]{4,2,3,1,0:T(8,128)} %copy.38), channel_id=1, source_target_pairs={{1,0},{3,2},{5,4},{7,6},{9,8},{11,10},{13,12},{15,14},{17,16},{19,... | collective-permute-start | bytes 589832 | tf_op jit(solution)/shard_map/ppermute | solution.py:22
  116.0 2.2 slice-start
  116.3 2.7 slice-start.1
  116.3 2.7 copy-start.4
  128.5 1.6 copy-start.1
  128.5 1.6 copy-start.2
  130.2 1.9 copy-start
  131.3 89.4 %all-gather.14.cloned.1.call-start = ((), (), s32[]{:S(2)}) async-start(), calls=%async_computation.3 | async-start | bytes 3342336 | tf_op jit(solution)/shard_map/all_gather | solution.py:28
  132.0 134.6 %all-gather.10.cloned.1.call-start = ((), (), s32[]{:S(2)}) async-start(), calls=%async_computation.1 | async-start | bytes 3342336 | tf_op jit(solution)/shard_map/all_gather | solution.py:28
Sparse Core Ops, SparseCore 0:
  9.5 77.0 all-gather.7
  131.4 43.1 all-gather.11
  176.9 43.7 all-gather.13
  222.8 43.7 all-gather.9
where the time goes:
time: 314 us; the launch traced here: 313 us
  waiting for transfers between devices  199 us (63%)
  other arithmetic  52.4 us (17%)
  local copies, waits for them, and re-layouts  34.5 us (11%)
  between operations  13.4 us (4%)
  starting transfers between devices  12.9 us (4%)
    all_gather x3, waiting for transfers between devices, joined(): gathered = jax.tree.map(lambda a: lax.all_gather(a, axis), part)  132 us
    all_gather x1, waiting for transfers between devices, local(): lax.all_gather(latest_model_output, 'date', axis=4, tiled=True)  62.8 us
    add x15, other arithmetic, combine(): left[2] * left_scale + right[2] * right_scale  18.7 us
    add x15, other arithmetic, combine(): left[1] * left_scale + right[1] * right_scale  18.6 us
    slice x3, local copies, waits for them, and re-layouts, extended(): last = lax.slice_in_dim(x, length - width, length, axis=dim)  16.3 us
    ppermute x2, starting transfers between devices, extended(): before = lax.ppermute(last, axis, up)  10 us
    reduce_sum x1, other arithmetic, cycle_distance(): jnp.sum(feature_discrepancy * feature_discrepancy * input_variable_scalin...  9.21 us
    all_gather x1, local copies, waits for them, and re-layouts, local(): lax.all_gather(latest_model_output, 'date', axis=4, tiled=True)  7.22 us
  transfers between devices with their start and end apart: 8, of which 5 were waited for; matrix products, arithmetic and copies ran while one was open for 10% of the time, Pallas kernels for 0%

commit v1 on v0

v1 whole, which is shorter than its diff:
```python
import math

import jax
import jax.numpy as jnp
from jax import lax
from jax.experimental import pallas as pl
from jax.experimental.pallas import tpu as pltpu
from jax.sharding import PartitionSpec as P

WIN_HALF = 3
LANES = 128
season_gain = 0.5


def season_term(calendar, today):
    return season_gain * (
        1.0 - jnp.cos(2.0 * math.pi * (calendar - today).astype(jnp.float32) / 365.0)
    )


def swap(x, mask):
    size = lax.axis_size("date")
    return lax.ppermute(x, "date", [(i, i ^ mask) for i in range(size)])


def pack_forecast(latest):
    cycles, leads, variables, rows, cols = latest.shape
    points = cycles * variables * rows
    flat = jnp.transpose(latest, (0, 2, 3, 4, 1)).reshape(points * cols, leads)
    groups = points // LANES

    def kernel(in_ref, out_ref, wide_ref):
        wide_ref[:, 0:leads] = in_ref[...]
        for group in range(groups):
            for col in range(cols):
                start = group * LANES * cols + col
                part = wide_ref[pl.ds(start, LANES, stride=cols), :].T
                out_ref[group, col * leads : (col + 1) * leads, :] = part[0:leads]

    return pl.pallas_call(
        kernel,
        out_shape=jax.ShapeDtypeStruct((groups, cols * leads, LANES), jnp.float32),
        scratch_shapes=[pltpu.VMEM((points * cols, LANES), jnp.float32)],
        name="pack_forecast",
    )(flat)


def pack_archive(past, pack):
    dates, leads, variables, rows, cols = past.shape
    if pack == 1:
        return past
    step = 4 if leads % 4 == 0 else 1

    def kernel(*refs):
        refs[pack][...] = jnp.concatenate([ref[...] for ref in refs[:pack]], axis=-1)

    def spec(j):
        return pl.BlockSpec(
            (1, step, variables, rows, cols), lambda p, t: (p * pack + j, t, 0, 0, 0)
        )

    return pl.pallas_call(
        kernel,
        grid=(dates // pack, leads // step),
        in_specs=[spec(j) for j in range(pack)],
        out_specs=pl.BlockSpec(
            (1, step, variables, rows, pack * cols), lambda p, t: (p, t, 0, 0, 0)
        ),
        out_shape=jax.ShapeDtypeStruct(
            (dates // pack, leads, variables, rows, pack * cols), jnp.float32
        ),
        name="pack_archive",
    )(*[past] * pack)


def gather_forecast(own):
    size = lax.axis_size("date")
    blocks = {0: own}
    far = list(range(4, size, 4))
    for mask in far:
        blocks[mask] = swap(own, mask)
    blocks[2] = swap(own, 2)
    for mask in far:
        blocks[mask ^ 2] = swap(blocks[mask], 2)
    for mask in range(0, size, 2):
        blocks[mask ^ 1] = swap(blocks[mask], 1)
    return blocks


def shifted(x, axis, step):
    zero = jnp.zeros_like(lax.slice_in_dim(x, 0, abs(step), axis=axis))
    length = x.shape[axis]
    if step > 0:
        return jnp.concatenate([zero, lax.slice_in_dim(x, 0, length - step, axis=axis)], axis)
    return jnp.concatenate([lax.slice_in_dim(x, -step, length, axis=axis), zero], axis)


def window_kernel(masks, dims, place_ref, weight_ref, *refs):
    cycles, sets, leads, variables, rows, cols, block = dims
    pieces = refs[: len(masks)]
    past_ref, out_ref, edge_ref, field_ref, diff_ref, sem = refs[len(masks) :]
    copies = []
    for k, mask in enumerate(masks):
        start = pl.multiple_of((place_ref[0] ^ mask) * block, 8)
        copies.append(
            pltpu.make_async_copy(pieces[k], field_ref.at[:, pl.ds(start, block)], sem.at[k])
        )
    for copy in copies:
        copy.start()
    for copy in copies:
        copy.wait()
    groups = field_ref.shape[0]
    pack = LANES // cols
    per_group = LANES // rows

    def one_lead(lead, carry):
        fields = []
        for group in range(groups):
            now = field_ref[group, pl.ds(lead, cols, stride=leads), :]
            fields.append(jnp.concatenate([now] * pack, axis=0).T)
        for s in range(sets):
            totals = [None] * cycles
            for v in range(variables):
                past = past_ref[s, lead, v]
                for c in range(cycles):
                    k = c * variables + v
                    at = (k % per_group) * rows
                    gap = fields[k // per_group][at : at + rows] - past
                    term = gap * gap * weight_ref[v]
                    totals[c] = term if v == 0 else totals[c] + term
            for c in range(cycles):
                diff_ref[c * sets + s, lead] = totals[c]
        return carry

    lax.fori_loop(0, leads, one_lead, 0)
    lane = lax.broadcasted_iota(jnp.int32, (rows, LANES), 1) % cols
    zero = jnp.zeros((rows, LANES), jnp.float32)
    for k in range(cycles * sets):
        a = [diff_ref[k, t] for t in range(leads)]
        for t in range(leads):
            total = None
            for u in range(max(0, t - WIN_HALF), min(leads, t + WIN_HALF + 1)):
                total = a[u] if total is None else total + a[u]
            left = jnp.where(lane == 0, zero, pltpu.roll(total, 1, 1))
            right = jnp.where(lane == cols - 1, zero, pltpu.roll(total, LANES - 1, 1))
            at = (k * leads + t) * rows
            out_ref[at : at + rows, :] = total + left + right
    for k in range(cycles * sets):
        first = out_ref[pl.ds(k * leads * rows, leads, stride=rows), :]
        last = out_ref[pl.ds(k * leads * rows + rows - 1, leads, stride=rows), :]
        edge_ref[0, k * leads : (k + 1) * leads, :] = first
        edge_ref[1, k * leads : (k + 1) * leads, :] = last


def partial_kernel(dims, scale, place_ref, season_ref, spread_ref, sum_ref, above_ref, below_ref, report_ref, out_ref, rows_ref):
    cycles, sets, leads, rows, cols, own = dims
    pack = LANES // cols
    line = lax.broadcasted_iota(jnp.int32, (rows, LANES), 0)
    lane = lax.broadcasted_iota(jnp.int32, (rows, LANES), 1)
    at_first = jnp.logical_and(line == 0, place_ref[0] > 0)
    at_last = jnp.logical_and(line == rows - 1, place_ref[0] < place_ref[1] - 1)
    zero = jnp.zeros((rows, LANES), jnp.float32)
    seasons = []
    for k in range(cycles * sets):
        season = jnp.full((rows, LANES), season_ref[k * pack], jnp.float32)
        for j in range(1, pack):
            season = jnp.where(lane >= j * cols, season_ref[k * pack + j], season)
        seasons.append(season)

    def across(x, combine):
        total = x
        for j in range(1, pack):
            total = combine(total, pltpu.roll(x, j * cols, 1))
        return total

    def one(c, lead):
        gaps = []
        for s in range(sets):
            k = (c * sets + s) * leads + lead
            mid = sum_ref[pl.ds(pl.multiple_of(k * rows, 8), rows), :]
            above = above_ref[pl.ds(k, rows, stride=0), :]
            below = below_ref[pl.ds(k, rows, stride=0), :]
            up = jnp.where(line == 0, jnp.where(at_first, above, zero), pltpu.roll(mid, 1, 0))
            down = jnp.where(
                line == rows - 1, jnp.where(at_last, below, zero), pltpu.roll(mid, rows - 1, 0)
            )
            gaps.append((mid + up + down) * scale + seasons[c * sets + s])
        low = gaps[0]
        for gap in gaps[1:]:
            low = jnp.minimum(low, gap)
        low = across(low, jnp.minimum)
        spread = spread_ref[lead]
        numer = denom = None
        for s in range(sets):
            weight = jnp.exp((low - gaps[s]) / spread)
            report = [report_ref[s * pack + j, lead] for j in range(pack)]
            term = weight * (report[0] if pack == 1 else jnp.concatenate(report, axis=-1))
            numer = term if s == 0 else numer + term
            denom = weight if s == 0 else denom + weight
        numer, denom = across(numer, jnp.add), across(denom, jnp.add)
        start = c * rows * leads + lead
        rows_ref[0, pl.ds(start, rows, stride=leads), :] = numer / denom
        rows_ref[1, pl.ds(start, rows, stride=leads), :] = low - spread * jnp.log(denom)

    def body(lead, carry):
        for c in range(cycles):
            one(c, lead)
        return carry

    lax.fori_loop(0, leads, body, 0)
    for k in range(2):
        whole = rows_ref[k].T
        for source in range(cols // own):
            out_ref[source, k * own : (k + 1) * own, :] = whole[source * own : (source + 1) * own]


def merge_kernel(dims, spread_ref, part_ref, out_ref):
    size, own, leads, groups = dims
    low = part_ref[0, own : 2 * own, :]
    for k in range(1, size):
        low = jnp.minimum(low, part_ref[k, own : 2 * own, :])
    numer = denom = None
    for k in range(size):
        weight = jnp.exp((low - part_ref[k, own : 2 * own, :]) / spread_ref[...])
        term = weight * part_ref[k, 0:own, :]
        numer = term if k == 0 else numer + term
        denom = weight if k == 0 else denom + weight
    ratio = numer / denom
    for g in range(groups):
        out_ref[g] = ratio[:, g * leads : (g + 1) * leads]


def local(
    latest_model_output,
    bygone_model_outputs,
    sensor_reports,
    input_variable_scaling,
    stepahead_blur_scale,
    bygone_annual_ordinal,
    launch_annual_ordinal,
):
    cycles, leads, variables, rows, own = latest_model_output.shape
    dates, _, _, _, cols = bygone_model_outputs.shape
    size, tiles = lax.axis_size("date"), lax.axis_size("tile")
    smem = pl.BlockSpec(memory_space=pltpu.SMEM)
    vmem = pl.BlockSpec(memory_space=pltpu.VMEM)
    anywhere = pl.BlockSpec(memory_space=pl.ANY)
    pack = max(1, LANES // cols)
    sets = dates // pack
    block = own * leads
    count = cycles * sets * leads

    blocks = gather_forecast(pack_forecast(latest_model_output))
    masks = sorted(blocks)
    place = lax.axis_index("date").astype(jnp.int32).reshape(1)
    past = pack_archive(bygone_model_outputs, pack)
    dims = (cycles, sets, leads, variables, rows, cols, block)
    sums, edges = pl.pallas_call(
        lambda *refs: window_kernel(masks, dims, *refs),
        out_shape=(
            jax.ShapeDtypeStruct((count * rows, LANES), jnp.float32),
            jax.ShapeDtypeStruct((2, count, LANES), jnp.float32),
        ),
        in_specs=[smem, smem] + [anywhere] * len(masks) + [vmem],
        out_specs=(vmem, vmem),
        scratch_shapes=[
            pltpu.VMEM((cycles * variables * rows // LANES, cols * leads, LANES), jnp.float32),
            pltpu.VMEM((cycles * sets, leads, rows, LANES), jnp.float32),
            pltpu.SemaphoreType.DMA((len(masks),)),
        ],
        name="window_sums",
    )(place, input_variable_scaling, *[blocks[m] for m in masks], past)

    tile_place = lax.axis_index("tile").astype(jnp.int32)
    if tiles == 2:
        sent = jnp.where(tile_place == 0, edges[1], edges[0])
        above = below = lax.ppermute(sent, "tile", [(0, 1), (1, 0)])
    else:
        above = lax.ppermute(edges[1], "tile", [(i, i + 1) for i in range(tiles - 1)])
        below = lax.ppermute(edges[0], "tile", [(i + 1, i) for i in range(tiles - 1)])
    season = season_term(bygone_annual_ordinal[None, :], launch_annual_ordinal[:, None]).reshape(-1)
    scale = 1.0 / (variables * 9.0 * (2 * WIN_HALF + 1))
    points = cycles * rows * leads
    partial = pl.pallas_call(
        lambda *refs: partial_kernel((cycles, sets, leads, rows, cols, own), scale, *refs),
        out_shape=jax.ShapeDtypeStruct((size, 2 * own, points), jnp.float32),
        in_specs=[smem, smem, smem] + [vmem] * 4,
        out_specs=vmem,
        scratch_shapes=[pltpu.VMEM((2, points, LANES), jnp.float32)],
        name="partial_mean",
    )(
        jnp.stack([tile_place, jnp.int32(tiles)]),
        season,
        stepahead_blur_scale,
        sums,
        above,
        below,
        sensor_reports,
    )
    parts = lax.all_to_all(partial, "date", 0, 0)
    spread = jnp.tile(stepahead_blur_scale, cycles * rows)[None, :]
    groups = cycles * rows
    merged = pl.pallas_call(
        lambda *refs: merge_kernel((size, own, leads, groups), *refs),
        out_shape=jax.ShapeDtypeStruct((groups, own, leads), jnp.float32),
        in_specs=[vmem, vmem],
        out_specs=vmem,
        name="merge_parts",
    )(spread, parts)
    return jnp.transpose(merged.reshape(cycles, rows, own, leads), (0, 3, 1, 2))


def solution(mesh):
    placed = (
        P(None, None, None, "tile", "date"),
        P("date", None, None, "tile", None),
        P("date", None, "tile", None),
        P(),
        P(),
        P("date"),
        P(),
    )
    return jax.shard_map(
        local, mesh=mesh, in_specs=placed, out_specs=P(None, None, "tile", "date"), check_vma=False
    )
```

time: 314 us -> 70.2 us (0.22)
  waiting for transfers between devices: 199 us -> 17.8 us
  other arithmetic: 52.4 us -> 2.22 us
  local copies, waits for them, and re-layouts: 34.5 us -> 3.34 us
  Pallas kernels: 0 us -> 25.9 us
  between operations: 13.4 us -> 0.25 us
  starting transfers between devices: 12.9 us -> 20 us
    all_gather x4 -> x0, waiting for transfers between devices: 195 us -> none  [the longest x3 132 us: joined(): gathered = jax.tree.map(lambda a: lax.all_gather(a, axis), part)]
    add x34 -> x0, other arithmetic: 38.4 us -> none  [the longest x15 18.7 us: combine(): left[2] * left_scale + right[2] * right_scale]
    pallas_call x0 -> x5, Pallas kernels: none -> 25.9 us  [the longest x1 9.1 us: pack_archive(): pl.pallas_call(kernel, grid=(dates // pack, leads // step), in_specs=[spe...]
    slice x5 -> x0, local copies, waits for them, and re-layouts: 18.6 us -> none  [the longest x3 16.3 us: extended(): last = lax.slice_in_dim(x, length - width, length, axis=dim)]
    reduce_sum x2 -> x0, other arithmetic: 10.3 us -> none  [the longest x1 9.21 us: cycle_distance(): jnp.sum(feature_discrepancy * feature_discrepancy * input_variable_scalin...]
    all_to_all x0 -> x1, waiting for transfers between devices: none -> 8.26 us  [local(): parts = lax.all_to_all(partial, 'date', 0, 0)]
    all_gather x1 -> x0, local copies, waits for them, and re-layouts: 7.22 us -> none  [local(): lax.all_gather(latest_model_output, 'date', axis=4, tiled=True)]
    all_to_all x0 -> x1, starting transfers between devices: none -> 6.57 us  [local(): parts = lax.all_to_all(partial, 'date', 0, 0)]
  transfers between devices with their start and end apart: 8 -> 17, of which waited for: 5 -> 6; matrix products, arithmetic and copies ran while one was open for 10% -> 4% of each run, Pallas kernels for 0% -> 13%
where the time goes in v1:
time: 70.2 us; the launch traced here: 69.6 us
  Pallas kernels  25.9 us (37%)
  starting transfers between devices  20 us (28%)
  waiting for transfers between devices  17.8 us (25%)
  local copies, waits for them, and re-layouts  3.34 us (5%)
  other arithmetic  2.22 us (3%)
    ppermute x15, starting transfers between devices, swap(): return lax.ppermute(x, 'date', [(i, i ^ mask) for i in range(size)])  12 us
    pallas_call x1, Pallas kernels, pack_archive(): pl.pallas_call(kernel, grid=(dates // pack, leads // step), in_specs=[spe...  9.1 us
    all_to_all x1, waiting for transfers between devices, local(): parts = lax.all_to_all(partial, 'date', 0, 0)  8.26 us
    ppermute x15, waiting for transfers between devices, swap(): return lax.ppermute(x, 'date', [(i, i ^ mask) for i in range(size)])  8.14 us
    pallas_call x1, Pallas kernels, local(): pl.pallas_call(lambda *refs: window_kernel(masks, dims, *refs), out_shape...  7.16 us
    all_to_all x1, starting transfers between devices, local(): parts = lax.all_to_all(partial, 'date', 0, 0)  6.57 us
    pallas_call x1, Pallas kernels, local(): pl.pallas_call(lambda *refs: partial_kernel((cycles, sets, leads, rows, c...  6.08 us
    unnamed x36, local copies, waits for them, and re-layouts  2.07 us
  transfers between devices with their start and end apart: 17, of which 6 were waited for; matrix products, arithmetic and copies ran while one was open for 4% of the time, Pallas kernels for 13%

profile of v1, /device:TPU:0, one launch (start us, length us, event | category | flops | bytes accessed | tf_op | source)
XLA Modules:
  0.0 69.6 jit_solution(820626614040703275)
XLA Ops:
  0.0 1.9 %pack_forecast.1.refs_2_ = f32[2,96,128]{2,1,0:T(8,128)} custom-call(f32[1024,24]{1,0:T(8,128)} %bitcast.10), custom_call_target="tpu_custom_call" | custom-call | tf_op jit(solution)/shard_map/pack_forecast/pallas_call | solution.py:40
  1.9 4.1 %collective-permute-start.7 = (f32[2,96,128]{2,1,0:T(8,128)}, f32[2,96,128]{2,1,0:T(8,128)S(1)}, u32[]{:S(2)}, u32[]{:S(2)}) collective-permute-start(f32[2,96,128]{2,1,0:T(8,128)} %pack_forecast.1.refs_2_), channel_id=1, source_target_pairs={{0,16},{2,18},{4,20},{6,22},{8,24},{10,26},{12,28},{14,30},{16,0},... | collective-permute-start | bytes 294920 | tf_op jit(solution)/shard_map/ppermute | solution.py:23
  5.9 1.3 %collective-permute-start.11 = (f32[2,96,128]{2,1,0:T(8,128)}, f32[2,96,128]{2,1,0:T(8,128)S(1)}, u32[]{:S(2)}, u32[]{:S(2)}) collective-permute-start(f32[2,96,128]{2,1,0:T(8,128)} %pack_forecast.1.refs_2_), channel_id=1, source_target_pairs={{0,24},{2,26},{4,28},{6,30},{8,16},{10,18},{12,20},{14,22},{16,8},... | collective-permute-start | bytes 294920 | tf_op jit(solution)/shard_map/ppermute | solution.py:23
  7.5 1.5 %collective-permute-start.1 = (f32[2,96,128]{2,1,0:T(8,128)}, f32[2,96,128]{2,1,0:T(8,128)S(1)}, u32[]{:S(2)}, u32[]{:S(2)}) collective-permute-start(f32[2,96,128]{2,1,0:T(8,128)} %pack_forecast.1.refs_2_), channel_id=1, source_target_pairs={{0,4},{2,6},{4,0},{6,2},{8,12},{10,14},{12,8},{14,10},{16,20},{18,... | collective-permute-start | bytes 294920 | tf_op jit(solution)/shard_map/ppermute | solution.py:23
  9.0 5.0 %collective-permute-done.7.refs_10_ = f32[2,96,128]{2,1,0:T(8,128)S(1)} collective-permute-done((f32[2,96,128]{2,1,0:T(8,128)}, f32[2,96,128]{2,1,0:T(8,128)S(1)}, u32[]{:S(2)}, u32[]{:S(2)}) %collective-permute-start.7) | collective-permute-done | bytes 98336 | tf_op jit(solution)/shard_map/ppermute | solution.py:23
  14.1 1.7 %collective-permute-start.9 = (f32[2,96,128]{2,1,0:T(8,128)S(1)}, f32[2,96,128]{2,1,0:T(8,128)S(1)}, u32[]{:S(2)}, u32[]{:S(2)}) collective-permute-start(f32[2,96,128]{2,1,0:T(8,128)S(1)} %collective-permute-done.7.refs_10_), channel_id=1, source_target_pairs={{0,4},{2,6},{4,0},{6,2},{8,12},{10,14},{12,8},{14,10},{16,20},{18,... | collective-permute-start | bytes 294920 | tf_op jit(solution)/shard_map/ppermute | solution.py:23
  16.1 1.7 %collective-permute-start.5 = (f32[2,96,128]{2,1,0:T(8,128)S(1)}, f32[2,96,128]{2,1,0:T(8,128)S(1)}, u32[]{:S(2)}, u32[]{:S(2)}) collective-permute-start(f32[2,96,128]{2,1,0:T(8,128)S(1)} %collective-permute-done.3.refs_6_), channel_id=1, source_target_pairs={{0,4},{2,6},{4,0},{6,2},{8,12},{10,14},{12,8},{14,10},{16,20},{18,... | collective-permute-start | bytes 294920 | tf_op jit(solution)/shard_map/ppermute | solution.py:23
  18.7 1.7 %collective-permute-done.13.refs_16_ = f32[2,96,128]{2,1,0:T(8,128)S(1)} collective-permute-done((f32[2,96,128]{2,1,0:T(8,128)S(1)}, f32[2,96,128]{2,1,0:T(8,128)S(1)}, u32[]{:S(2)}, u32[]{:S(2)}) %collective-permute-start.13) | collective-permute-done | bytes 98336 | tf_op jit(solution)/shard_map/ppermute | solution.py:23
  20.4 1.0 %collective-permute-done.5.refs_8_ = f32[2,96,128]{2,1,0:T(8,128)S(1)} collective-permute-done((f32[2,96,128]{2,1,0:T(8,128)S(1)}, f32[2,96,128]{2,1,0:T(8,128)S(1)}, u32[]{:S(2)}, u32[]{:S(2)}) %collective-permute-start.5) | collective-permute-done | bytes 98336 | tf_op jit(solution)/shard_map/ppermute | solution.py:23
  22.1 0.8 %subtract_multiply_fusion = f32[2,4]{1,0:T(2,128)S(1)} fusion(s32[4]{0:T(128)} %param.12, s32[2]{0:T(128)} %param.13), kind=kLoop, calls=%fused_computation.1 | loop fusion | flops 40 | bytes 56 | tf_op jit(solution)/shard_map/mul | solution.py:16
  22.8 9.1 %pack_archive.1.refs_18_ = f32[2,24,16,8,128]{4,3,2,1,0:T(8,128)} custom-call(f32[4,24,16,8,64]{4,3,2,1,0:T(8,128)} %refs_1_.2, f32[4,24,16,8,64]{4,3,2,1,0:T(8,128)} %refs_1_.2), custom_call_target="tpu_custom_call" | custom-call | tf_op jit(solution)/shard_map/pack_archive/pallas_call | solution.py:62
  32.9 7.2 %window_sums.1 = (f32[768,128]{1,0:T(8,128)}, f32[2,96,128]{2,1,0:T(8,128)}) custom-call(s32[1]{0:T(128)} %bitcast.1.refs_0_, f32[16]{0:T(128)} %refs_1_.3, f32[2,96,128]{2,1,0:T(8,128)} %pack_forecast.1.refs_2_, f32[2,96,128]{2,1,0:T(8,128)} %copy-done.6, f32[2,96,128]{2,1,0:T(8,128)} %copy-done.5, f32[2,96,128]{2,1,0:T(8,128)} %copy-done.13, ...), custom_call_target="tpu_custom_call" | custom-call | tf_op jit(solution)/shard_map/window_sums/pallas_call | solution.py:258
  40.0 0.8 %select_bitcast_fusion = f32[96,128]{1,0:T(8,128)S(1)} fusion(f32[2,96,128]{2,1,0:T(8,128)} %get-tuple-element.8, pred[]{:T(512)S(6)} %eq.3), kind=kLoop, calls=%fused_computation | loop fusion | flops 12288 | bytes 147457 | tf_op jit(solution)/shard_map/jit(_where)/select_n | solution.py:276
  40.9 1.5 %collective-permute-start.15 = (f32[96,128]{1,0:T(8,128)S(1)}, f32[96,128]{1,0:T(8,128)S(1)}, u32[]{:S(2)}, u32[]{:S(2)}) collective-permute-start(f32[96,128]{1,0:T(8,128)S(1)} %select_bitcast_fusion), channel_id=1, source_target_pairs={{0,1},{1,0},{2,3},{3,2},{4,5},{5,4},{6,7},{7,6},{8,9},{9,8},{10,11... | collective-permute-start | bytes 147464 | tf_op jit(solution)/shard_map/ppermute | solution.py:277
  42.4 0.6 pad_add_fusion.refs_0_
  43.0 0.6 reshape.28.refs_1_
  43.6 1.4 %collective-permute-done.15.refs_4_.refs_5_ = f32[96,128]{1,0:T(8,128)S(1)} collective-permute-done((f32[96,128]{1,0:T(8,128)S(1)}, f32[96,128]{1,0:T(8,128)S(1)}, u32[]{:S(2)}, u32[]{:S(2)}) %collective-permute-start.15) | collective-permute-done | bytes 49184 | tf_op jit(solution)/shard_map/ppermute | solution.py:277
  45.0 0.6 copy-done.1
  45.6 6.1 %partial_mean.1 = f32[16,8,384]{2,1,0:T(8,128)} custom-call(s32[2]{0:T(128)} %pad_add_fusion.refs_0_, f32[8]{0:T(128)} %reshape.28.refs_1_, f32[24]{0:T(128)} %refs_2_.1, f32[768,128]{1,0:T(8,128)} %get-tuple-element.7.refs_3_, f32[96,128]{1,0:T(8,128)} %copy-done.1, f32[96,128]{1,0:T(8,128)} %copy-done.1, f32[4,24,8,64]{3,2,1,0:T(8,128)} %refs_6_.1), custom_call_target="tpu_custom_call" | custom-call | tf_op jit(solution)/shard_map/partial_mean/pallas_call | solution.py:284
  51.7 6.6 %all-to-all-start = ((f32[16,8,384]{2,1,0:T(8,128)}), f32[16,8,384]{2,1,0:T(8,128)S(1)}, u32[]{:S(2)}, u32[]{:S(2)}) async-start(f32[16,8,384]{2,1,0:T(8,128)} %partial_mean.1), calls=%async_computation | async-start | bytes 393216 | tf_op jit(solution)/shard_map/all_to_all | solution.py:300
  58.3 0.7 broadcast_in_dim_tile.3.refs_0_
  58.9 8.3 %all-to-all-done.refs_1_ = f32[16,8,384]{2,1,0:T(8,128)S(1)} async-done(((f32[16,8,384]{2,1,0:T(8,128)}), f32[16,8,384]{2,1,0:T(8,128)S(1)}, u32[]{:S(2)}, u32[]{:S(2)}) %all-to-all-start) | async-done | bytes 196640 | tf_op jit(solution)/shard_map/all_to_all | solution.py:300
  67.2 0.7 copy-done
  67.9 1.7 %merge_parts.1 = f32[16,4,24]{2,1,0:T(4,128)} custom-call(f32[1,384]{1,0:T(1,128)} %broadcast_in_dim_tile.3.refs_0_, f32[16,8,384]{2,1,0:T(8,128)} %copy-done), custom_call_target="tpu_custom_call" | custom-call | tf_op jit(solution)/shard_map/merge_parts/pallas_call | solution.py:303
  (57 shorter events, 2.8 us)
Async XLA Ops:
  1.9 12.2 %collective-permute-start.7 = (f32[2,96,128]{2,1,0:T(8,128)}, f32[2,96,128]{2,1,0:T(8,128)S(1)}, u32[]{:S(2)}, u32[]{:S(2)}) collective-permute-start(f32[2,96,128]{2,1,0:T(8,128)} %pack_forecast.1.refs_2_), channel_id=1, source_target_pairs={{0,16},{2,18},{4,20},{6,22},{8,24},{10,26},{12,28},{14,30},{16,0},... | collective-permute-start | bytes 294920 | tf_op jit(solution)/shard_map/ppermute | solution.py:23
  5.9 9.8 %collective-permute-start.11 = (f32[2,96,128]{2,1,0:T(8,128)}, f32[2,96,128]{2,1,0:T(8,128)S(1)}, u32[]{:S(2)}, u32[]{:S(2)}) collective-permute-start(f32[2,96,128]{2,1,0:T(8,128)} %pack_forecast.1.refs_2_), channel_id=1, source_target_pairs={{0,24},{2,26},{4,28},{6,30},{8,16},{10,18},{12,20},{14,22},{16,8},... | collective-permute-start | bytes 294920 | tf_op jit(solution)/shard_map/ppermute | solution.py:23
  7.3 8.8 %collective-permute-start.3 = (f32[2,96,128]{2,1,0:T(8,128)}, f32[2,96,128]{2,1,0:T(8,128)S(1)}, u32[]{:S(2)}, u32[]{:S(2)}) collective-permute-start(f32[2,96,128]{2,1,0:T(8,128)} %pack_forecast.1.refs_2_), channel_id=1, source_target_pairs={{0,8},{2,10},{4,12},{6,14},{8,0},{10,2},{12,4},{14,6},{16,24},{18,... | collective-permute-start | bytes 294920 | tf_op jit(solution)/shard_map/ppermute | solution.py:23
  7.5 10.3 %collective-permute-start.1 = (f32[2,96,128]{2,1,0:T(8,128)}, f32[2,96,128]{2,1,0:T(8,128)S(1)}, u32[]{:S(2)}, u32[]{:S(2)}) collective-permute-start(f32[2,96,128]{2,1,0:T(8,128)} %pack_forecast.1.refs_2_), channel_id=1, source_target_pairs={{0,4},{2,6},{4,0},{6,2},{8,12},{10,14},{12,8},{14,10},{16,20},{18,... | collective-permute-start | bytes 294920 | tf_op jit(solution)/shard_map/ppermute | solution.py:23
  9.0 8.8 %collective-permute-start = (f32[2,96,128]{2,1,0:T(8,128)}, f32[2,96,128]{2,1,0:T(8,128)S(1)}, u32[]{:S(2)}, u32[]{:S(2)}) collective-permute-start(f32[2,96,128]{2,1,0:T(8,128)} %pack_forecast.1.refs_2_), channel_id=1, source_target_pairs={{0,2},{2,0},{4,6},{6,4},{8,10},{10,8},{12,14},{14,12},{16,18},{18,... | collective-permute-start | bytes 294920 | tf_op jit(solution)/shard_map/ppermute | solution.py:23
  14.0 17.9 %copy-start.2 = (f32[2,96,128]{2,1,0:T(8,128)}, f32[2,96,128]{2,1,0:T(8,128)S(1)}, u32[]{:S(2)}) copy-start(f32[2,96,128]{2,1,0:T(8,128)S(1)} %collective-permute-done.7.refs_10_) | copy-start | bytes 294916
  14.1 4.6 %collective-permute-start.9 = (f32[2,96,128]{2,1,0:T(8,128)S(1)}, f32[2,96,128]{2,1,0:T(8,128)S(1)}, u32[]{:S(2)}, u32[]{:S(2)}) collective-permute-start(f32[2,96,128]{2,1,0:T(8,128)S(1)} %collective-permute-done.7.refs_10_), channel_id=1, source_target_pairs={{0,4},{2,6},{4,0},{6,2},{8,12},{10,14},{12,8},{14,10},{16,20},{18,... | collective-permute-start | bytes 294920 | tf_op jit(solution)/shard_map/ppermute | solution.py:23
  15.8 16.2 %copy-start.3 = (f32[2,96,128]{2,1,0:T(8,128)}, f32[2,96,128]{2,1,0:T(8,128)S(1)}, u32[]{:S(2)}) copy-start(f32[2,96,128]{2,1,0:T(8,128)S(1)} %collective-permute-done.11.refs_14_) | copy-start | bytes 294916
  15.8 4.6 %collective-permute-start.13 = (f32[2,96,128]{2,1,0:T(8,128)S(1)}, f32[2,96,128]{2,1,0:T(8,128)S(1)}, u32[]{:S(2)}, u32[]{:S(2)}) collective-permute-start(f32[2,96,128]{2,1,0:T(8,128)S(1)} %collective-permute-done.11.refs_14_), channel_id=1, source_target_pairs={{0,4},{2,6},{4,0},{6,2},{8,12},{10,14},{12,8},{14,10},{16,20},{18,... | collective-permute-start | bytes 294920 | tf_op jit(solution)/shard_map/ppermute | solution.py:23
  16.1 15.9 %copy-start.4 = (f32[2,96,128]{2,1,0:T(8,128)}, f32[2,96,128]{2,1,0:T(8,128)S(1)}, u32[]{:S(2)}) copy-start(f32[2,96,128]{2,1,0:T(8,128)S(1)} %collective-permute-done.3.refs_6_) | copy-start | bytes 294916
  16.1 5.3 %collective-permute-start.5 = (f32[2,96,128]{2,1,0:T(8,128)S(1)}, f32[2,96,128]{2,1,0:T(8,128)S(1)}, u32[]{:S(2)}, u32[]{:S(2)}) collective-permute-start(f32[2,96,128]{2,1,0:T(8,128)S(1)} %collective-permute-done.3.refs_6_), channel_id=1, source_target_pairs={{0,4},{2,6},{4,0},{6,2},{8,12},{10,14},{12,8},{14,10},{16,20},{18,... | collective-permute-start | bytes 294920 | tf_op jit(solution)/shard_map/ppermute | solution.py:23
  17.8 14.2 %copy-start.5 = (f32[2,96,128]{2,1,0:T(8,128)}, f32[2,96,128]{2,1,0:T(8,128)S(1)}, u32[]{:S(2)}) copy-start(f32[2,96,128]{2,1,0:T(8,128)S(1)} %collective-permute-done.1.refs_4_) | copy-start | bytes 294916
  17.8 3.6 %collective-permute-start.12 = (f32[2,96,128]{2,1,0:T(8,128)S(1)}, f32[2,96,128]{2,1,0:T(8,128)S(1)}, u32[]{:S(2)}, u32[]{:S(2)}) collective-permute-start(f32[2,96,128]{2,1,0:T(8,128)S(1)} %collective-permute-done.11.refs_14_), channel_id=1, source_target_pairs={{0,2},{2,0},{4,6},{6,4},{8,10},{10,8},{12,14},{14,12},{16,18},{18,... | collective-permute-start | bytes 294920 | tf_op jit(solution)/shard_map/ppermute | solution.py:23
  17.8 14.1 %copy-start.6 = (f32[2,96,128]{2,1,0:T(8,128)}, f32[2,96,128]{2,1,0:T(8,128)S(1)}, u32[]{:S(2)}) copy-start(f32[2,96,128]{2,1,0:T(8,128)S(1)} %collective-permute-done.refs_3_) | copy-start | bytes 294916
  17.8 4.1 %collective-permute-start.4 = (f32[2,96,128]{2,1,0:T(8,128)S(1)}, f32[2,96,128]{2,1,0:T(8,128)S(1)}, u32[]{:S(2)}, u32[]{:S(2)}) collective-permute-start(f32[2,96,128]{2,1,0:T(8,128)S(1)} %collective-permute-done.3.refs_6_), channel_id=1, source_target_pairs={{0,2},{2,0},{4,6},{6,4},{8,10},{10,8},{12,14},{14,12},{16,18},{18,... | collective-permute-start | bytes 294920 | tf_op jit(solution)/shard_map/ppermute | solution.py:23
  18.7 13.3 %copy-start.7 = (f32[2,96,128]{2,1,0:T(8,128)}, f32[2,96,128]{2,1,0:T(8,128)S(1)}, u32[]{:S(2)}) copy-start(f32[2,96,128]{2,1,0:T(8,128)S(1)} %collective-permute-done.9.refs_12_) | copy-start | bytes 294916
  18.7 13.4 %collective-permute-start.8 = (f32[2,96,128]{2,1,0:T(8,128)S(1)}, f32[2,96,128]{2,1,0:T(8,128)S(1)}, u32[]{:S(2)}, u32[]{:S(2)}) collective-permute-start(f32[2,96,128]{2,1,0:T(8,128)S(1)} %collective-permute-done.7.refs_10_), channel_id=1, source_target_pairs={{0,2},{2,0},{4,6},{6,4},{8,10},{10,8},{12,14},{14,12},{16,18},{18,... | collective-permute-start | bytes 294920 | tf_op jit(solution)/shard_map/ppermute | solution.py:23
  20.4 11.7 %collective-permute-start.2 = (f32[2,96,128]{2,1,0:T(8,128)S(1)}, f32[2,96,128]{2,1,0:T(8,128)S(1)}, u32[]{:S(2)}, u32[]{:S(2)}) collective-permute-start(f32[2,96,128]{2,1,0:T(8,128)S(1)} %collective-permute-done.1.refs_4_), channel_id=1, source_target_pairs={{0,2},{2,0},{4,6},{6,4},{8,10},{10,8},{12,14},{14,12},{16,18},{18,... | collective-permute-start | bytes 294920 | tf_op jit(solution)/shard_map/ppermute | solution.py:23
  21.4 10.6 %collective-permute-start.10 = (f32[2,96,128]{2,1,0:T(8,128)S(1)}, f32[2,96,128]{2,1,0:T(8,128)S(1)}, u32[]{:S(2)}, u32[]{:S(2)}) collective-permute-start(f32[2,96,128]{2,1,0:T(8,128)S(1)} %collective-permute-done.9.refs_12_), channel_id=1, source_target_pairs={{0,2},{2,0},{4,6},{6,4},{8,10},{10,8},{12,14},{14,12},{16,18},{18,... | collective-permute-start | bytes 294920 | tf_op jit(solution)/shard_map/ppermute | solution.py:23
  21.5 10.6 %collective-permute-start.14 = (f32[2,96,128]{2,1,0:T(8,128)S(1)}, f32[2,96,128]{2,1,0:T(8,128)S(1)}, u32[]{:S(2)}, u32[]{:S(2)}) collective-permute-start(f32[2,96,128]{2,1,0:T(8,128)S(1)} %collective-permute-done.13.refs_16_), channel_id=1, source_target_pairs={{0,2},{2,0},{4,6},{6,4},{8,10},{10,8},{12,14},{14,12},{16,18},{18,... | collective-permute-start | bytes 294920 | tf_op jit(solution)/shard_map/ppermute | solution.py:23
  22.0 10.2 %collective-permute-start.6 = (f32[2,96,128]{2,1,0:T(8,128)S(1)}, f32[2,96,128]{2,1,0:T(8,128)S(1)}, u32[]{:S(2)}, u32[]{:S(2)}) collective-permute-start(f32[2,96,128]{2,1,0:T(8,128)S(1)} %collective-permute-done.5.refs_8_), channel_id=1, source_target_pairs={{0,2},{2,0},{4,6},{6,4},{8,10},{10,8},{12,14},{14,12},{16,18},{18,... | collective-permute-start | bytes 294920 | tf_op jit(solution)/shard_map/ppermute | solution.py:23
  32.0 26.2 %copy-start.17 = (f32[24]{0:T(128)S(1)}, f32[24]{0:T(128)}, u32[]{:S(2)}) copy-start(f32[24]{0:T(128)} %refs_2_.1) | copy-start | bytes 292
  40.9 4.1 %collective-permute-start.15 = (f32[96,128]{1,0:T(8,128)S(1)}, f32[96,128]{1,0:T(8,128)S(1)}, u32[]{:S(2)}, u32[]{:S(2)}) collective-permute-start(f32[96,128]{1,0:T(8,128)S(1)} %select_bitcast_fusion), channel_id=1, source_target_pairs={{0,1},{1,0},{2,3},{3,2},{4,5},{5,4},{6,7},{7,6},{8,9},{9,8},{10,11... | collective-permute-start | bytes 147464 | tf_op jit(solution)/shard_map/ppermute | solution.py:277
  51.7 15.5 %all-to-all-start = ((f32[16,8,384]{2,1,0:T(8,128)}), f32[16,8,384]{2,1,0:T(8,128)S(1)}, u32[]{:S(2)}, u32[]{:S(2)}) async-start(f32[16,8,384]{2,1,0:T(8,128)} %partial_mean.1), calls=%async_computation | async-start | bytes 393216 | tf_op jit(solution)/shard_map/all_to_all | solution.py:300
  (11 other events, 47.5 us)

commit v2 on v1

--- a/solution.py
+++ b/solution.py
@@ -9,6 +9,7 @@
 
 WIN_HALF = 3
 LANES = 128
+KERNEL_PARAMS = pltpu.CompilerParams(vmem_limit_bytes=16 * 2**20)
 season_gain = 0.5
 
 
@@ -41,36 +42,10 @@
         kernel,
         out_shape=jax.ShapeDtypeStruct((groups, cols * leads, LANES), jnp.float32),
         scratch_shapes=[pltpu.VMEM((points * cols, LANES), jnp.float32)],
+        cost_estimate=pl.CostEstimate(flops=10**10, transcendentals=0, bytes_accessed=10**6),
+        compiler_params=KERNEL_PARAMS,
         name="pack_forecast",
     )(flat)
-
-
-def pack_archive(past, pack):
-    dates, leads, variables, rows, cols = past.shape
-    if pack == 1:
-        return past
-    step = 4 if leads % 4 == 0 else 1
-
-    def kernel(*refs):
-        refs[pack][...] = jnp.concatenate([ref[...] for ref in refs[:pack]], axis=-1)
-
-    def spec(j):
-        return pl.BlockSpec(
-            (1, step, variables, rows, cols), lambda p, t: (p * pack + j, t, 0, 0, 0)
-        )
-
-    return pl.pallas_call(
-        kernel,
-        grid=(dates // pack, leads // step),
-        in_specs=[spec(j) for j in range(pack)],
-        out_specs=pl.BlockSpec(
-            (1, step, variables, rows, pack * cols), lambda p, t: (p, t, 0, 0, 0)
-        ),
-        out_shape=jax.ShapeDtypeStruct(
-            (dates // pack, leads, variables, rows, pack * cols), jnp.float32
-        ),
-        name="pack_archive",
-    )(*[past] * pack)
 
 
 def gather_forecast(own):
@@ -95,20 +70,16 @@
     return jnp.concatenate([lax.slice_in_dim(x, -step, length, axis=axis), zero], axis)
 
 
-def window_kernel(masks, dims, place_ref, weight_ref, *refs):
+def window_kernel(masks, dims, weight_ref, *refs):
     cycles, sets, leads, variables, rows, cols, block = dims
     pieces = refs[: len(masks)]
-    past_ref, out_ref, edge_ref, field_ref, diff_ref, sem = refs[len(masks) :]
-    copies = []
+    past_ref, out_ref = refs[len(masks) : len(masks) + 2]
+    edge_refs = refs[len(masks) + 2 : -2]
+    field_ref, diff_ref = refs[-2:]
+    place = lax.axis_index("date")
     for k, mask in enumerate(masks):
-        start = pl.multiple_of((place_ref[0] ^ mask) * block, 8)
-        copies.append(
-            pltpu.make_async_copy(pieces[k], field_ref.at[:, pl.ds(start, block)], sem.at[k])
-        )
-    for copy in copies:
-        copy.start()
-    for copy in copies:
-        copy.wait()
+        start = pl.multiple_of((place ^ mask) * block, 8)
+        field_ref[:, pl.ds(start, block), :] = pieces[k][...]
     groups = field_ref.shape[0]
     pack = LANES // cols
     per_group = LANES // rows
@@ -121,7 +92,10 @@
         for s in range(sets):
             totals = [None] * cycles
             for v in range(variables):
-                past = past_ref[s, lead, v]
+                past = past_ref[s * pack, lead, v]
+                if pack > 1:
+                    more = [past_ref[s * pack + j, lead, v] for j in range(1, pack)]
+                    past = jnp.concatenate([past] + more, axis=-1)
                 for c in range(cycles):
                     k = c * variables + v
                     at = (k % per_group) * rows
@@ -148,17 +122,23 @@
     for k in range(cycles * sets):
         first = out_ref[pl.ds(k * leads * rows, leads, stride=rows), :]
         last = out_ref[pl.ds(k * leads * rows + rows - 1, leads, stride=rows), :]
-        edge_ref[0, k * leads : (k + 1) * leads, :] = first
-        edge_ref[1, k * leads : (k + 1) * leads, :] = last
-
-
-def partial_kernel(dims, scale, place_ref, season_ref, spread_ref, sum_ref, above_ref, below_ref, report_ref, out_ref, rows_ref):
+        if len(edge_refs) == 1:
+            edge_refs[0][k * leads : (k + 1) * leads, :] = jnp.where(
+                lax.axis_index("tile") == 0, last, first
+            )
+        else:
+            edge_refs[0][k * leads : (k + 1) * leads, :] = first
+            edge_refs[1][k * leads : (k + 1) * leads, :] = last
+
+
+def partial_kernel(dims, scale, season_ref, spread_ref, sum_ref, above_ref, below_ref, report_ref, out_ref, rows_ref):
     cycles, sets, leads, rows, cols, own = dims
     pack = LANES // cols
     line = lax.broadcasted_iota(jnp.int32, (rows, LANES), 0)
     lane = lax.broadcasted_iota(jnp.int32, (rows, LANES), 1)
-    at_first = jnp.logical_and(line == 0, place_ref[0] > 0)
-    at_last = jnp.logical_and(line == rows - 1, place_ref[0] < place_ref[1] - 1)
+    place, tiles = lax.axis_index("tile"), lax.axis_size("tile")
+    at_first = jnp.logical_and(line == 0, place > 0)
+    at_last = jnp.logical_and(line == rows - 1, place < tiles - 1)
     zero = jnp.zeros((rows, LANES), jnp.float32)
     seasons = []
     for k in range(cycles * sets):
@@ -207,7 +187,7 @@
             one(c, lead)
         return carry
 
-    lax.fori_loop(0, leads, body, 0)
+    lax.fori_loop(0, leads, body, 0, unroll=4)
     for k in range(2):
         whole = rows_ref[k].T
         for source in range(cols // own):
@@ -244,7 +224,6 @@
     size, tiles = lax.axis_size("date"), lax.axis_size("tile")
     smem = pl.BlockSpec(memory_space=pltpu.SMEM)
     vmem = pl.BlockSpec(memory_space=pltpu.VMEM)
-    anywhere = pl.BlockSpec(memory_space=pl.ANY)
     pack = max(1, LANES // cols)
     sets = dates // pack
     block = own * leads
@@ -252,29 +231,27 @@
 
     blocks = gather_forecast(pack_forecast(latest_model_output))
     masks = sorted(blocks)
-    place = lax.axis_index("date").astype(jnp.int32).reshape(1)
-    past = pack_archive(bygone_model_outputs, pack)
     dims = (cycles, sets, leads, variables, rows, cols, block)
-    sums, edges = pl.pallas_call(
+    edge = jax.ShapeDtypeStruct((count, LANES), jnp.float32)
+    edge_count = 1 if tiles == 2 else 2
+    sums, *edges = pl.pallas_call(
         lambda *refs: window_kernel(masks, dims, *refs),
         out_shape=(
             jax.ShapeDtypeStruct((count * rows, LANES), jnp.float32),
-            jax.ShapeDtypeStruct((2, count, LANES), jnp.float32),
+            *[edge] * edge_count,
         ),
-        in_specs=[smem, smem] + [anywhere] * len(masks) + [vmem],
-        out_specs=(vmem, vmem),
+        in_specs=[smem] + [vmem] * len(masks) + [vmem],
+        out_specs=(vmem,) * (1 + edge_count),
         scratch_shapes=[
             pltpu.VMEM((cycles * variables * rows // LANES, cols * leads, LANES), jnp.float32),
             pltpu.VMEM((cycles * sets, leads, rows, LANES), jnp.float32),
-            pltpu.SemaphoreType.DMA((len(masks),)),
         ],
+        compiler_params=KERNEL_PARAMS,
         name="window_sums",
-    )(place, input_variable_scaling, *[blocks[m] for m in masks], past)
-
-    tile_place = lax.axis_index("tile").astype(jnp.int32)
+    )(input_variable_scaling, *[blocks[m] for m in masks], bygone_model_outputs)
+
     if tiles == 2:
-        sent = jnp.where(tile_place == 0, edges[1], edges[0])
-        above = below = lax.ppermute(sent, "tile", [(0, 1), (1, 0)])
+        above = below = lax.ppermute(edges[0], "tile", [(0, 1), (1, 0)])
     else:
         above = lax.ppermute(edges[1], "tile", [(i, i + 1) for i in range(tiles - 1)])
         below = lax.ppermute(edges[0], "tile", [(i + 1, i) for i in range(tiles - 1)])
@@ -284,12 +261,12 @@
     partial = pl.pallas_call(
         lambda *refs: partial_kernel((cycles, sets, leads, rows, cols, own), scale, *refs),
         out_shape=jax.ShapeDtypeStruct((size, 2 * own, points), jnp.float32),
-        in_specs=[smem, smem, smem] + [vmem] * 4,
+        in_specs=[smem, smem] + [vmem] * 4,
         out_specs=vmem,
         scratch_shapes=[pltpu.VMEM((2, points, LANES), jnp.float32)],
+        compiler_params=KERNEL_PARAMS,
         name="partial_mean",
     )(
-        jnp.stack([tile_place, jnp.int32(tiles)]),
         season,
         stepahead_blur_scale,
         sums,
@@ -305,6 +282,7 @@
         out_shape=jax.ShapeDtypeStruct((groups, own, leads), jnp.float32),
         in_specs=[vmem, vmem],
         out_specs=vmem,
+        compiler_params=KERNEL_PARAMS,
         name="merge_parts",
     )(spread, parts)
     return jnp.transpose(merged.reshape(cycles, rows, own, leads), (0, 3, 1, 2))

time: 70.2 us -> 50.7 us (0.72)
  Pallas kernels: 25.9 us -> 8.37 us
  waiting for transfers between devices: 17.8 us -> 20.4 us
  other arithmetic: 2.22 us -> 0.11 us
  local copies, waits for them, and re-layouts: 3.34 us -> 1.24 us
    pallas_call x1 -> x0, Pallas kernels: 9.1 us -> none  [pack_archive(): pl.pallas_call(kernel, grid=(dates // pack, leads // step), in_specs=[spe...]
    pallas_call x1, Pallas kernels: 6.08 us -> 2.51 us  [local(): pl.pallas_call(lambda *refs: partial_kernel((cycles, sets, leads, rows, c...]
    pallas_call x1, Pallas kernels: 7.16 us -> 4.92 us  [local(): pl.pallas_call(lambda *refs: window_kernel(masks, dims, *refs), out_shape...]
    pallas_call x1, Pallas kernels: 1.87 us -> 0.16 us  [pack_forecast(): pl.pallas_call(kernel, out_shape=jax.ShapeDtypeStruct((groups, cols * lea...]
    ppermute x15, waiting for transfers between devices: 8.14 us -> 9.16 us  [swap(): return lax.ppermute(x, 'date', [(i, i ^ mask) for i in range(size)])]
    unnamed x36 -> x14, local copies, waits for them, and re-layouts: 2.07 us -> 1.07 us
    ppermute x1, waiting for transfers between devices: 1.4 us -> 2.4 us  [local(): above = below = lax.ppermute(edges[0], 'tile', [(0, 1), (1, 0)])]
    pallas_call x1, Pallas kernels: 1.71 us -> 0.78 us  [local(): pl.pallas_call(lambda *refs: merge_kernel((size, own, leads, groups), *re...]
  transfers between devices with their start and end apart: 17 -> 17, of which waited for: 6 -> 9; matrix products, arithmetic and copies ran while one was open for 4% -> 1% of each run, Pallas kernels for 13% -> 0%
where the time goes in v2:
time: 50.7 us; the launch traced here: 50.4 us
  waiting for transfers between devices  20.4 us (40%)
  starting transfers between devices  20.2 us (40%)
  Pallas kernels  8.37 us (17%)
  local copies, waits for them, and re-layouts  1.24 us (2%)
    ppermute x15, starting transfers between devices, swap(): return lax.ppermute(x, 'date', [(i, i ^ mask) for i in range(size)])  12.1 us
    ppermute x15, waiting for transfers between devices, swap(): return lax.ppermute(x, 'date', [(i, i ^ mask) for i in range(size)])  9.16 us
    all_to_all x1, waiting for transfers between devices, local(): parts = lax.all_to_all(partial, 'date', 0, 0)  8.86 us
    all_to_all x1, starting transfers between devices, local(): parts = lax.all_to_all(partial, 'date', 0, 0)  6.57 us
    pallas_call x1, Pallas kernels, local(): pl.pallas_call(lambda *refs: window_kernel(masks, dims, *refs), out_shape...  4.92 us
    pallas_call x1, Pallas kernels, local(): pl.pallas_call(lambda *refs: partial_kernel((cycles, sets, leads, rows, c...  2.51 us
    ppermute x1, waiting for transfers between devices, local(): above = below = lax.ppermute(edges[0], 'tile', [(0, 1), (1, 0)])  2.4 us
    ppermute x1, starting transfers between devices, local(): above = below = lax.ppermute(edges[0], 'tile', [(0, 1), (1, 0)])  1.56 us
  transfers between devices with their start and end apart: 17, of which 9 were waited for; matrix products, arithmetic and copies ran while one was open for 1% of the time, Pallas kernels for 0%

profile of v2, /device:TPU:0, one launch (start us, length us, event | category | flops | bytes accessed | tf_op | source)
XLA Modules:
  0.0 50.4 jit_solution(3556381441654949367)
XLA Ops:
  0.0 1.0 %copy-done.4 = f32[2,24,16,8,4]{1,4,3,2,0:T(4,128)S(1)} copy-done((f32[2,24,16,8,4]{1,4,3,2,0:T(4,128)S(1)}, f32[2,24,16,8,4]{1,4,3,2,0:T(4,128)}, u32[]{:S(2)}) %copy-start.4) | copy-done | bytes 98328
  1.2 4.1 %collective-permute-start.7 = (f32[2,96,128]{2,1,0:T(8,128)S(1)}, f32[2,96,128]{2,1,0:T(8,128)S(1)}, u32[]{:S(2)}, u32[]{:S(2)}) collective-permute-start(f32[2,96,128]{2,1,0:T(8,128)S(1)} %pack_forecast.1.refs_1_), channel_id=1, source_target_pairs={{0,16},{2,18},{4,20},{6,22},{8,24},{10,26},{12,28},{14,30},{16,0},... | collective-permute-start | bytes 294920 | tf_op jit(solution)/shard_map/ppermute | solution.py:24
  5.4 1.3 %collective-permute-start.11 = (f32[2,96,128]{2,1,0:T(8,128)S(1)}, f32[2,96,128]{2,1,0:T(8,128)S(1)}, u32[]{:S(2)}, u32[]{:S(2)}) collective-permute-start(f32[2,96,128]{2,1,0:T(8,128)S(1)} %pack_forecast.1.refs_1_), channel_id=1, source_target_pairs={{0,24},{2,26},{4,28},{6,30},{8,16},{10,18},{12,20},{14,22},{16,8},... | collective-permute-start | bytes 294920 | tf_op jit(solution)/shard_map/ppermute | solution.py:24
  6.7 0.2 collective-permute-start.3
  7.0 1.5 %collective-permute-start.1 = (f32[2,96,128]{2,1,0:T(8,128)S(1)}, f32[2,96,128]{2,1,0:T(8,128)S(1)}, u32[]{:S(2)}, u32[]{:S(2)}) collective-permute-start(f32[2,96,128]{2,1,0:T(8,128)S(1)} %pack_forecast.1.refs_1_), channel_id=1, source_target_pairs={{0,4},{2,6},{4,0},{6,2},{8,12},{10,14},{12,8},{14,10},{16,20},{18,... | collective-permute-start | bytes 294920 | tf_op jit(solution)/shard_map/ppermute | solution.py:24
  8.5 4.8 %collective-permute-done.7.refs_9_ = f32[2,96,128]{2,1,0:T(8,128)S(1)} collective-permute-done((f32[2,96,128]{2,1,0:T(8,128)S(1)}, f32[2,96,128]{2,1,0:T(8,128)S(1)}, u32[]{:S(2)}, u32[]{:S(2)}) %collective-permute-start.7) | collective-permute-done | bytes 98336 | tf_op jit(solution)/shard_map/ppermute | solution.py:24
  13.3 1.7 %collective-permute-start.9 = (f32[2,96,128]{2,1,0:T(8,128)S(1)}, f32[2,96,128]{2,1,0:T(8,128)S(1)}, u32[]{:S(2)}, u32[]{:S(2)}) collective-permute-start(f32[2,96,128]{2,1,0:T(8,128)S(1)} %collective-permute-done.7.refs_9_), channel_id=1, source_target_pairs={{0,4},{2,6},{4,0},{6,2},{8,12},{10,14},{12,8},{14,10},{16,20},{18,... | collective-permute-start | bytes 294920 | tf_op jit(solution)/shard_map/ppermute | solution.py:24
  15.0 0.3 collective-permute-start.13
  15.3 1.7 %collective-permute-start.5 = (f32[2,96,128]{2,1,0:T(8,128)S(1)}, f32[2,96,128]{2,1,0:T(8,128)S(1)}, u32[]{:S(2)}, u32[]{:S(2)}) collective-permute-start(f32[2,96,128]{2,1,0:T(8,128)S(1)} %collective-permute-done.3.refs_5_), channel_id=1, source_target_pairs={{0,4},{2,6},{4,0},{6,2},{8,12},{10,14},{12,8},{14,10},{16,20},{18,... | collective-permute-start | bytes 294920 | tf_op jit(solution)/shard_map/ppermute | solution.py:24
  17.0 0.5 %collective-permute-start.4 = (f32[2,96,128]{2,1,0:T(8,128)S(1)}, f32[2,96,128]{2,1,0:T(8,128)S(1)}, u32[]{:S(2)}, u32[]{:S(2)}) collective-permute-start(f32[2,96,128]{2,1,0:T(8,128)S(1)} %collective-permute-done.3.refs_5_), channel_id=1, source_target_pairs={{0,2},{2,0},{4,6},{6,4},{8,10},{10,8},{12,14},{14,12},{16,18},{18,... | collective-permute-start | bytes 294920 | tf_op jit(solution)/shard_map/ppermute | solution.py:24
  17.5 0.4 collective-permute-done.9.refs_11_
  17.9 1.7 %collective-permute-done.13.refs_15_ = f32[2,96,128]{2,1,0:T(8,128)S(1)} collective-permute-done((f32[2,96,128]{2,1,0:T(8,128)S(1)}, f32[2,96,128]{2,1,0:T(8,128)S(1)}, u32[]{:S(2)}, u32[]{:S(2)}) %collective-permute-start.13) | collective-permute-done | bytes 98336 | tf_op jit(solution)/shard_map/ppermute | solution.py:24
  19.6 1.0 %collective-permute-done.5.refs_7_ = f32[2,96,128]{2,1,0:T(8,128)S(1)} collective-permute-done((f32[2,96,128]{2,1,0:T(8,128)S(1)}, f32[2,96,128]{2,1,0:T(8,128)S(1)}, u32[]{:S(2)}, u32[]{:S(2)}) %collective-permute-start.5) | collective-permute-done | bytes 98336 | tf_op jit(solution)/shard_map/ppermute | solution.py:24
  20.7 0.5 %collective-permute-start.14 = (f32[2,96,128]{2,1,0:T(8,128)S(1)}, f32[2,96,128]{2,1,0:T(8,128)S(1)}, u32[]{:S(2)}, u32[]{:S(2)}) collective-permute-start(f32[2,96,128]{2,1,0:T(8,128)S(1)} %collective-permute-done.13.refs_15_), channel_id=1, source_target_pairs={{0,2},{2,0},{4,6},{6,4},{8,10},{10,8},{12,14},{14,12},{16,18},{18,... | collective-permute-start | bytes 294920 | tf_op jit(solution)/shard_map/ppermute | solution.py:24
  21.3 0.7 %collective-permute-done.10.refs_12_ = f32[2,96,128]{2,1,0:T(8,128)S(1)} collective-permute-done((f32[2,96,128]{2,1,0:T(8,128)S(1)}, f32[2,96,128]{2,1,0:T(8,128)S(1)}, u32[]{:S(2)}, u32[]{:S(2)}) %collective-permute-start.10) | collective-permute-done | bytes 98336 | tf_op jit(solution)/shard_map/ppermute | solution.py:24
  22.0 0.2 collective-permute-done.14.refs_16_
  22.1 0.4 collective-permute-done.6.refs_8_
  22.5 4.9 %window_sums.1 = (f32[768,128]{1,0:T(8,128)S(1)}, f32[96,128]{1,0:T(8,128)S(1)}) custom-call(f32[16]{0:T(128)S(1)} %copy-done.3, f32[2,96,128]{2,1,0:T(8,128)S(1)} %pack_forecast.1.refs_1_, f32[2,96,128]{2,1,0:T(8,128)S(1)} %collective-permute-done.refs_2_, f32[2,96,128]{2,1,0:T(8,128)S(1)} %collective-permute-done.1.refs_3_, ...), custom_call_target="tpu_custom_call" | custom-call | tf_op jit(solution)/shard_map/window_sums/pallas_call | solution.py:237
  27.4 1.6 %collective-permute-start.15 = (f32[96,128]{1,0:T(8,128)S(1)}, f32[96,128]{1,0:T(8,128)S(1)}, u32[]{:S(2)}, u32[]{:S(2)}) collective-permute-start(f32[96,128]{1,0:T(8,128)S(1)} %get-tuple-element.8), channel_id=1, source_target_pairs={{0,1},{1,0},{2,3},{3,2},{4,5},{5,4},{6,7},{7,6},{8,9},{9,8},{10,11... | collective-permute-start | bytes 147464 | tf_op jit(solution)/shard_map/ppermute | solution.py:254
  29.2 2.4 %collective-permute-done.15.refs_3_.refs_4_ = f32[96,128]{1,0:T(8,128)S(1)} collective-permute-done((f32[96,128]{1,0:T(8,128)S(1)}, f32[96,128]{1,0:T(8,128)S(1)}, u32[]{:S(2)}, u32[]{:S(2)}) %collective-permute-start.15) | collective-permute-done | bytes 49184 | tf_op jit(solution)/shard_map/ppermute | solution.py:254
  31.6 2.5 %partial_mean.1 = f32[16,8,384]{2,1,0:T(8,128)} custom-call(f32[8]{0:T(128)S(1)} %reshape.22.refs_0_, f32[24]{0:T(128)S(1)} %copy-done.2, f32[768,128]{1,0:T(8,128)S(1)} %get-tuple-element.7.refs_2_, f32[96,128]{1,0:T(8,128)S(1)} %collective-permute-done.15.refs_3_.refs_4_, f32[96,128]{1,0:T(8,128)S(1)} %collective-permute-done.15.refs_3_.refs_4_, ...), custom_call_target="tpu_custom_call" | custom-call | tf_op jit(solution)/shard_map/partial_mean/pallas_call | solution.py:261
  34.1 6.6 %all-to-all-start = ((f32[16,8,384]{2,1,0:T(8,128)}), f32[16,8,384]{2,1,0:T(8,128)S(1)}, u32[]{:S(2)}, u32[]{:S(2)}) async-start(f32[16,8,384]{2,1,0:T(8,128)} %partial_mean.1), calls=%async_computation | async-start | bytes 393216 | tf_op jit(solution)/shard_map/all_to_all | solution.py:277
  40.8 8.9 %all-to-all-done.refs_1_ = f32[16,8,384]{2,1,0:T(8,128)S(1)} async-done(((f32[16,8,384]{2,1,0:T(8,128)}), f32[16,8,384]{2,1,0:T(8,128)S(1)}, u32[]{:S(2)}, u32[]{:S(2)}) %all-to-all-start) | async-done | bytes 196640 | tf_op jit(solution)/shard_map/all_to_all | solution.py:277
  49.6 0.8 %merge_parts.1 = f32[16,4,24]{2,1,0:T(4,128)} custom-call(f32[1,384]{1,0:T(1,128)S(1)} %broadcast_in_dim_tile.3.refs_0_, f32[16,8,384]{2,1,0:T(8,128)S(1)} %all-to-all-done.refs_1_), custom_call_target="tpu_custom_call" | custom-call | tf_op jit(solution)/shard_map/merge_parts/pallas_call | solution.py:280
  (32 shorter events, 0.6 us)
Async XLA Ops:
  0.0 1.0 %copy-start.4 = (f32[2,24,16,8,4]{1,4,3,2,0:T(4,128)S(1)}, f32[2,24,16,8,4]{1,4,3,2,0:T(4,128)}, u32[]{:S(2)}) copy-start(f32[2,24,16,8,4]{1,4,3,2,0:T(4,128)} %param.7) | copy-start | bytes 294916
  1.0 21.4 %copy-start = (f32[4,24,16,8,64]{4,3,2,1,0:T(8,128)S(1)}, f32[4,24,16,8,64]{4,3,2,1,0:T(8,128)}, u32[]{:S(2)}) copy-start(f32[4,24,16,8,64]{4,3,2,1,0:T(8,128)} %refs_17_.1) | copy-start | bytes 9437188
  1.0 21.4 %copy-start.3 = (f32[16]{0:T(128)S(1)}, f32[16]{0:T(128)}, u32[]{:S(2)}) copy-start(f32[16]{0:T(128)} %refs_0_.1) | copy-start | bytes 196
  1.2 27.8 %copy-start.5 = (s32[4]{0:T(128)S(1)}, s32[4]{0:T(128)}, u32[]{:S(2)}) copy-start(s32[4]{0:T(128)} %param.12) | copy-start | bytes 52
  1.2 27.8 %copy-start.6 = (s32[2]{0:T(128)S(1)}, s32[2]{0:T(128)}, u32[]{:S(2)}) copy-start(s32[2]{0:T(128)} %param.13) | copy-start | bytes 28
  1.2 30.4 %copy-start.1 = (f32[4,24,8,64]{3,2,1,0:T(8,128)S(1)}, f32[4,24,8,64]{3,2,1,0:T(8,128)}, u32[]{:S(2)}) copy-start(f32[4,24,8,64]{3,2,1,0:T(8,128)} %refs_5_.1) | copy-start | bytes 589828
  1.2 30.3 %copy-start.2 = (f32[24]{0:T(128)S(1)}, f32[24]{0:T(128)}, u32[]{:S(2)}) copy-start(f32[24]{0:T(128)} %refs_1_.1) | copy-start | bytes 292
  1.2 12.0 %collective-permute-start.7 = (f32[2,96,128]{2,1,0:T(8,128)S(1)}, f32[2,96,128]{2,1,0:T(8,128)S(1)}, u32[]{:S(2)}, u32[]{:S(2)}) collective-permute-start(f32[2,96,128]{2,1,0:T(8,128)S(1)} %pack_forecast.1.refs_1_), channel_id=1, source_target_pairs={{0,16},{2,18},{4,20},{6,22},{8,24},{10,26},{12,28},{14,30},{16,0},... | collective-permute-start | bytes 294920 | tf_op jit(solution)/shard_map/ppermute | solution.py:24
  5.4 9.6 %collective-permute-start.11 = (f32[2,96,128]{2,1,0:T(8,128)S(1)}, f32[2,96,128]{2,1,0:T(8,128)S(1)}, u32[]{:S(2)}, u32[]{:S(2)}) collective-permute-start(f32[2,96,128]{2,1,0:T(8,128)S(1)} %pack_forecast.1.refs_1_), channel_id=1, source_target_pairs={{0,24},{2,26},{4,28},{6,30},{8,16},{10,18},{12,20},{14,22},{16,8},... | collective-permute-start | bytes 294920 | tf_op jit(solution)/shard_map/ppermute | solution.py:24
  6.7 8.6 %collective-permute-start.3 = (f32[2,96,128]{2,1,0:T(8,128)S(1)}, f32[2,96,128]{2,1,0:T(8,128)S(1)}, u32[]{:S(2)}, u32[]{:S(2)}) collective-permute-start(f32[2,96,128]{2,1,0:T(8,128)S(1)} %pack_forecast.1.refs_1_), channel_id=1, source_target_pairs={{0,8},{2,10},{4,12},{6,14},{8,0},{10,2},{12,4},{14,6},{16,24},{18,... | collective-permute-start | bytes 294920 | tf_op jit(solution)/shard_map/ppermute | solution.py:24
  7.0 10.1 %collective-permute-start.1 = (f32[2,96,128]{2,1,0:T(8,128)S(1)}, f32[2,96,128]{2,1,0:T(8,128)S(1)}, u32[]{:S(2)}, u32[]{:S(2)}) collective-permute-start(f32[2,96,128]{2,1,0:T(8,128)S(1)} %pack_forecast.1.refs_1_), channel_id=1, source_target_pairs={{0,4},{2,6},{4,0},{6,2},{8,12},{10,14},{12,8},{14,10},{16,20},{18,... | collective-permute-start | bytes 294920 | tf_op jit(solution)/shard_map/ppermute | solution.py:24
  8.5 8.6 %collective-permute-start = (f32[2,96,128]{2,1,0:T(8,128)S(1)}, f32[2,96,128]{2,1,0:T(8,128)S(1)}, u32[]{:S(2)}, u32[]{:S(2)}) collective-permute-start(f32[2,96,128]{2,1,0:T(8,128)S(1)} %pack_forecast.1.refs_1_), channel_id=1, source_target_pairs={{0,2},{2,0},{4,6},{6,4},{8,10},{10,8},{12,14},{14,12},{16,18},{18,... | collective-permute-start | bytes 294920 | tf_op jit(solution)/shard_map/ppermute | solution.py:24
  13.3 4.6 %collective-permute-start.9 = (f32[2,96,128]{2,1,0:T(8,128)S(1)}, f32[2,96,128]{2,1,0:T(8,128)S(1)}, u32[]{:S(2)}, u32[]{:S(2)}) collective-permute-start(f32[2,96,128]{2,1,0:T(8,128)S(1)} %collective-permute-done.7.refs_9_), channel_id=1, source_target_pairs={{0,4},{2,6},{4,0},{6,2},{8,12},{10,14},{12,8},{14,10},{16,20},{18,... | collective-permute-start | bytes 294920 | tf_op jit(solution)/shard_map/ppermute | solution.py:24
  15.0 4.6 %collective-permute-start.13 = (f32[2,96,128]{2,1,0:T(8,128)S(1)}, f32[2,96,128]{2,1,0:T(8,128)S(1)}, u32[]{:S(2)}, u32[]{:S(2)}) collective-permute-start(f32[2,96,128]{2,1,0:T(8,128)S(1)} %collective-permute-done.11.refs_13_), channel_id=1, source_target_pairs={{0,4},{2,6},{4,0},{6,2},{8,12},{10,14},{12,8},{14,10},{16,20},{18,... | collective-permute-start | bytes 294920 | tf_op jit(solution)/shard_map/ppermute | solution.py:24
  15.3 5.3 %collective-permute-start.5 = (f32[2,96,128]{2,1,0:T(8,128)S(1)}, f32[2,96,128]{2,1,0:T(8,128)S(1)}, u32[]{:S(2)}, u32[]{:S(2)}) collective-permute-start(f32[2,96,128]{2,1,0:T(8,128)S(1)} %collective-permute-done.3.refs_5_), channel_id=1, source_target_pairs={{0,4},{2,6},{4,0},{6,2},{8,12},{10,14},{12,8},{14,10},{16,20},{18,... | collective-permute-start | bytes 294920 | tf_op jit(solution)/shard_map/ppermute | solution.py:24
  17.0 3.6 %collective-permute-start.12 = (f32[2,96,128]{2,1,0:T(8,128)S(1)}, f32[2,96,128]{2,1,0:T(8,128)S(1)}, u32[]{:S(2)}, u32[]{:S(2)}) collective-permute-start(f32[2,96,128]{2,1,0:T(8,128)S(1)} %collective-permute-done.11.refs_13_), channel_id=1, source_target_pairs={{0,2},{2,0},{4,6},{6,4},{8,10},{10,8},{12,14},{14,12},{16,18},{18,... | collective-permute-start | bytes 294920 | tf_op jit(solution)/shard_map/ppermute | solution.py:24
  17.0 4.1 %collective-permute-start.4 = (f32[2,96,128]{2,1,0:T(8,128)S(1)}, f32[2,96,128]{2,1,0:T(8,128)S(1)}, u32[]{:S(2)}, u32[]{:S(2)}) collective-permute-start(f32[2,96,128]{2,1,0:T(8,128)S(1)} %collective-permute-done.3.refs_5_), channel_id=1, source_target_pairs={{0,2},{2,0},{4,6},{6,4},{8,10},{10,8},{12,14},{14,12},{16,18},{18,... | collective-permute-start | bytes 294920 | tf_op jit(solution)/shard_map/ppermute | solution.py:24
  17.9 3.4 %collective-permute-start.8 = (f32[2,96,128]{2,1,0:T(8,128)S(1)}, f32[2,96,128]{2,1,0:T(8,128)S(1)}, u32[]{:S(2)}, u32[]{:S(2)}) collective-permute-start(f32[2,96,128]{2,1,0:T(8,128)S(1)} %collective-permute-done.7.refs_9_), channel_id=1, source_target_pairs={{0,2},{2,0},{4,6},{6,4},{8,10},{10,8},{12,14},{14,12},{16,18},{18,... | collective-permute-start | bytes 294920 | tf_op jit(solution)/shard_map/ppermute | solution.py:24
  19.6 1.6 %collective-permute-start.2 = (f32[2,96,128]{2,1,0:T(8,128)S(1)}, f32[2,96,128]{2,1,0:T(8,128)S(1)}, u32[]{:S(2)}, u32[]{:S(2)}) collective-permute-start(f32[2,96,128]{2,1,0:T(8,128)S(1)} %collective-permute-done.1.refs_3_), channel_id=1, source_target_pairs={{0,2},{2,0},{4,6},{6,4},{8,10},{10,8},{12,14},{14,12},{16,18},{18,... | collective-permute-start | bytes 294920 | tf_op jit(solution)/shard_map/ppermute | solution.py:24
  20.7 1.3 %collective-permute-start.10 = (f32[2,96,128]{2,1,0:T(8,128)S(1)}, f32[2,96,128]{2,1,0:T(8,128)S(1)}, u32[]{:S(2)}, u32[]{:S(2)}) collective-permute-start(f32[2,96,128]{2,1,0:T(8,128)S(1)} %collective-permute-done.9.refs_11_), channel_id=1, source_target_pairs={{0,2},{2,0},{4,6},{6,4},{8,10},{10,8},{12,14},{14,12},{16,18},{18,... | collective-permute-start | bytes 294920 | tf_op jit(solution)/shard_map/ppermute | solution.py:24
  20.7 1.5 %collective-permute-start.14 = (f32[2,96,128]{2,1,0:T(8,128)S(1)}, f32[2,96,128]{2,1,0:T(8,128)S(1)}, u32[]{:S(2)}, u32[]{:S(2)}) collective-permute-start(f32[2,96,128]{2,1,0:T(8,128)S(1)} %collective-permute-done.13.refs_15_), channel_id=1, source_target_pairs={{0,2},{2,0},{4,6},{6,4},{8,10},{10,8},{12,14},{14,12},{16,18},{18,... | collective-permute-start | bytes 294920 | tf_op jit(solution)/shard_map/ppermute | solution.py:24
  21.2 1.3 %collective-permute-start.6 = (f32[2,96,128]{2,1,0:T(8,128)S(1)}, f32[2,96,128]{2,1,0:T(8,128)S(1)}, u32[]{:S(2)}, u32[]{:S(2)}) collective-permute-start(f32[2,96,128]{2,1,0:T(8,128)S(1)} %collective-permute-done.5.refs_7_), channel_id=1, source_target_pairs={{0,2},{2,0},{4,6},{6,4},{8,10},{10,8},{12,14},{14,12},{16,18},{18,... | collective-permute-start | bytes 294920 | tf_op jit(solution)/shard_map/ppermute | solution.py:24
  27.4 4.2 %collective-permute-start.15 = (f32[96,128]{1,0:T(8,128)S(1)}, f32[96,128]{1,0:T(8,128)S(1)}, u32[]{:S(2)}, u32[]{:S(2)}) collective-permute-start(f32[96,128]{1,0:T(8,128)S(1)} %get-tuple-element.8), channel_id=1, source_target_pairs={{0,1},{1,0},{2,3},{3,2},{4,5},{5,4},{6,7},{7,6},{8,9},{9,8},{10,11... | collective-permute-start | bytes 147464 | tf_op jit(solution)/shard_map/ppermute | solution.py:254
  34.1 15.5 %all-to-all-start = ((f32[16,8,384]{2,1,0:T(8,128)}), f32[16,8,384]{2,1,0:T(8,128)S(1)}, u32[]{:S(2)}, u32[]{:S(2)}) async-start(f32[16,8,384]{2,1,0:T(8,128)} %partial_mean.1), calls=%async_computation | async-start | bytes 393216 | tf_op jit(solution)/shard_map/all_to_all | solution.py:277
